TPU v7x, 256 devices: a whole 4x4x8 slice. The times are simulated.
256 devices in a mesh: branch: 8 (over z), mp: 8 (over y_lo, x), dp: 4 (over y_hi, core).
Axes of the slice: x: 4, y: 4 (y_hi: 2, y_lo: 2; y = y_hi * 2 + y_lo), z: 8, core: 2. Of those that a mesh axis runs over, the one named last changes fastest.
Arguments:
- context: bfloat16 [4096, 4096], P(('branch', 'dp'), 'mp'), may hold values from -6 to 6
- residual: bfloat16 [4096, 4096], P(('branch', 'dp')), may hold values from -12 to 12
- attn_weight: bfloat16 [8, 4096, 4096], P('branch', 'mp', 'dp'), may hold values from -0.25 to 0.25
- norm_gain: bfloat16 [4096], replicated, may hold values from 0.099609375 to 1.8984375
- gate_weight: bfloat16 [8, 4096, 5504], P('branch', None, ('mp', 'dp')), may hold values from -0.09375 to 0.09375
- up_weight: bfloat16 [8, 4096, 5504], P('branch', None, ('mp', 'dp')), may hold values from -0.09375 to 0.09375
- down_weight: bfloat16 [8, 5504, 4096], P('branch', ('mp', 'dp')), may hold values from -0.078125 to 0.078125
- cotangent: bfloat16 [4096, 4096], P(('branch', 'dp')), may hold values from -0.796875 to 0.796875
- expert_ids: int32 [4096, 2], P(('branch', 'dp')), may hold values from 0 to 7, as said below
- gate_fixed: int32 [4096, 2], P(('branch', 'dp')), may hold values from 1 to 32767, as said below
Outputs:
- grad_gate: bfloat16 [8, 4096, 5504], P('branch', None, ('mp', 'dp'))
- grad_up: bfloat16 [8, 4096, 5504], P('branch', None, ('mp', 'dp'))
- grad_down: bfloat16 [8, 5504, 4096], P('branch', ('mp', 'dp'))
Inputs may be any that keep to these rules, and one draw needn't show every extreme that they name: `expert_ids`: the two entries of a row differ; in every aligned block of 128 rows some expert is named by more than 40 choices. `gate_fixed`: the two entries of a row sum to 32768.
All inputs are finite; a program needn't handle non-finite values.
Results may differ from a plain program's by a relative error of at most 0.025.
Values may be sent and summed in bfloat16 or wider, within the bound.
A program may use at most 128 MiB of HBM per device.

v0:
```python
import functools
import jax
import jax.numpy as jnp
from jax import lax
from jax.sharding import PartitionSpec as P


def slot_positions(id_block, capacity, experts):
    rows = id_block.shape[0]
    picks = jnp.concatenate([id_block[:, 0], id_block[:, 1]], axis=0)
    onehot = (picks[:, None] == jnp.arange(experts, dtype=jnp.int32)[None, :]).astype(jnp.int32)
    position = jnp.sum((jnp.cumsum(onehot, axis=0) - 1) * onehot, axis=1)
    position = jnp.where(position < capacity, position, -1)
    return jnp.stack([position[:rows], position[rows:]], axis=1)


def expert_pass(weight_set, totals, block_rows, first_row):
    w_gate, w_up, w_down = weight_set
    tokens_in, cotan_rows = block_rows
    pre_gate = jnp.dot(tokens_in, w_gate, preferred_element_type=jnp.float32)
    pre_up = jnp.dot(tokens_in, w_up, preferred_element_type=jnp.float32)
    sigmoid_gate = jax.nn.sigmoid(pre_gate)
    active = pre_gate * sigmoid_gate
    hidden = (active * pre_up).astype(jnp.bfloat16)
    back_grad = lax.dot_general(
        cotan_rows, w_down, (((1,), (1,)), ((), ())), preferred_element_type=jnp.float32
    )
    d_gate = (back_grad * pre_up * sigmoid_gate * (1.0 + pre_gate * (1.0 - sigmoid_gate))).astype(
        jnp.bfloat16
    )
    d_up = (back_grad * active).astype(jnp.bfloat16)
    contract = (((0,), (0,)), ((), ()))
    sum_gate = lax.dot_general(tokens_in, d_gate, contract, preferred_element_type=jnp.float32)
    sum_up = lax.dot_general(tokens_in, d_up, contract, preferred_element_type=jnp.float32)
    sum_down = lax.dot_general(hidden, cotan_rows, contract, preferred_element_type=jnp.float32)
    return (sum_gate, sum_up, sum_down)


def per_device(
    context,
    residual,
    attn_weight,
    norm_gain,
    gate_weight,
    up_weight,
    down_weight,
    cotangent,
    expert_ids,
    gate_fixed,
):
    branches = lax.axis_size("branch")
    summed = lax.psum(attn_weight[0].astype(jnp.float32).astype(jnp.bfloat16), "branch").astype(
        jnp.float32
    )
    merged = (summed / branches).astype(jnp.bfloat16)
    partial_out = jnp.dot(
        context,
        lax.all_gather(merged, "dp", axis=1, tiled=True),
        preferred_element_type=jnp.float32,
    ).astype(jnp.bfloat16)
    attention = lax.psum(partial_out.astype(jnp.float32).astype(jnp.bfloat16), "mp").astype(
        jnp.float32
    )
    mixed_in = residual.astype(jnp.float32) + attention
    inv_rms = lax.rsqrt(jnp.mean(mixed_in * mixed_in, axis=1, keepdims=True) + 1e-05)
    normed = (mixed_in * inv_rms * norm_gain.astype(jnp.float32)[None, :]).astype(jnp.bfloat16)
    model_width = residual.shape[1]
    group_tokens = residual.shape[0]
    experts = branches * gate_weight.shape[0]
    capacity = 5 * group_tokens // (2 * experts)
    slots = slot_positions(expert_ids, capacity, experts)
    slot_share = capacity // lax.axis_size("mp")
    offset = lax.axis_index("mp") * slot_share
    local_slot = slots - offset
    in_share = (slots >= 0) & (local_slot >= 0) & (local_slot < slot_share)
    slot_code = jnp.where(in_share, expert_ids * slot_share + local_slot, -1)
    target = jnp.arange(experts * slot_share, dtype=jnp.int32)
    matches = slot_code[None, :, :] == target[:, None, None]
    selector = jnp.any(matches, axis=2).astype(jnp.bfloat16)
    row_gate = jnp.sum(
        jnp.where(matches, gate_fixed[None, :, :].astype(jnp.float32) / 32768.0, 0.0), axis=(1, 2)
    )
    send_in = jnp.dot(selector, normed, preferred_element_type=jnp.float32).astype(jnp.bfloat16)
    send_in = send_in.reshape(experts, slot_share, model_width)
    cot_rows = jnp.dot(selector, cotangent, preferred_element_type=jnp.float32)
    send_cot = (
        (cot_rows * row_gate[:, None])
        .astype(jnp.bfloat16)
        .reshape(experts, slot_share, model_width)
    )
    hidden_width = gate_weight.shape[2]
    start_totals = (
        jnp.zeros((model_width, hidden_width), jnp.float32),
        jnp.zeros((model_width, hidden_width), jnp.float32),
        jnp.zeros((hidden_width, model_width), jnp.float32),
    )
    accumulate = functools.partial(expert_pass, (gate_weight[0], up_weight[0], down_weight[0]))
    routed_in, routed_cot = (
        lax.all_to_all(send_in, "branch", split_axis=0, concat_axis=1, tiled=True),
        lax.all_to_all(send_cot, "branch", split_axis=0, concat_axis=1, tiled=True),
    )
    totals = accumulate(
        start_totals,
        (
            lax.all_gather(routed_in[0], ("mp", "dp"), axis=0, tiled=True),
            lax.all_gather(routed_cot[0], ("mp", "dp"), axis=0, tiled=True),
        ),
        jnp.int32(0),
    )
    grad_gate = totals[0].astype(jnp.bfloat16)[None]
    grad_up = totals[1].astype(jnp.bfloat16)[None]
    grad_down = totals[2].astype(jnp.bfloat16)[None]
    return (grad_gate, grad_up, grad_down)


def solution(mesh):
    return jax.shard_map(
        per_device,
        mesh=mesh,
        in_specs=(
            P(("branch", "dp"), "mp"),
            P(("branch", "dp"), None),
            P("branch", "mp", "dp"),
            P(),
            P("branch", None, ("mp", "dp")),
            P("branch", None, ("mp", "dp")),
            P("branch", ("mp", "dp"), None),
            P(("branch", "dp"), None),
            P(("branch", "dp"), None),
            P(("branch", "dp"), None),
        ),
        out_specs=(
            P("branch", None, ("mp", "dp")),
            P("branch", None, ("mp", "dp")),
            P("branch", ("mp", "dp"), None),
        ),
        check_vma=False,
    )
```

profile of v0, /device:TPU:1, one launch (start us, length us, event | category | flops | bytes accessed | tf_op | source)
XLA Modules:
  0.0 354.2 jit_solution(13398183778796547387)
XLA Ops:
  8.1 0.7 all-reduce.3.cloned.1.call-update
  8.8 77.8 %all-reduce.3.cloned.1.call-done = bf16[512,1024]{1,0:T(8,128)(2,1)} async-done(((bf16[512,1024]{1,0:T(8,128)(2,1)}), bf16[512,1024]{1,0:T(8,128)(2,1)}) %all-reduce.3.cloned.1.call-update) | async-done | bytes 1048592 | tf_op jit(solution)/shard_map/psum | solution.py:52
  86.6 2.4 multiply_convert_fusion.1
  89.1 0.6 reduce-window.6
  89.7 0.2 slice_reduce_fusion
  90.1 43.3 %all-gather.4.cloned.1.call-done = bf16[512,4096]{1,0:T(8,128)(2,1)} async-done(((bf16[512,1024]{1,0:T(8,128)(2,1)}), bf16[512,4096]{1,0:T(8,128)(2,1)}) %all-gather.4.cloned.1.call-update) | async-done | bytes 4194320 | tf_op jit(solution)/shard_map/all_gather | solution.py:58
  133.5 4.5 %fusion.3 = bf16[128,4096]{0,1:T(8,128)(2,1)} fusion(bf16[512,4096]{1,0:T(8,128)(2,1)} %all-gather.4.cloned.1.call-done, bf16[128,512]{1,0:T(8,128)(2,1)S(1)} %copy-done.4), kind=kOutput, calls=%fused_computation.7 | convolution fusion | flops 537395200 | bytes 5373952 | tf_op jit(solution)/shard_map/dot_general | solution.py:56
  138.2 0.3 fusion.4
  138.6 24.0 %all_to_all.8 = bf16[8,5,4096]{2,1,0:T(8,128)(2,1)S(1)} all-to-all(bf16[8,5,4096]{2,1,0:T(8,128)(2,1)S(1)} %reshape.54), channel_id=1, replica_groups=mesh['branch'=8,'mp'=8,'dp'=4] {'branch'}, dimensions={0} | all-to-all | bytes 655360 | tf_op jit(solution)/shard_map/all_to_all | solution.py:100
  162.6 0.9 squeeze.28
  163.6 0.6 convert_element_type.69
  164.2 0.7 copy.19
  164.9 61.1 %all-reduce.5.cloned.1.call-done = bf16[128,4096]{0,1:T(8,128)(2,1)} async-done(((bf16[128,4096]{0,1:T(8,128)(2,1)}), bf16[128,4096]{0,1:T(8,128)(2,1)}) %all-reduce.5.cloned.1.call-update) | async-done | bytes 1048592 | tf_op jit(solution)/shard_map/psum | solution.py:61
  226.0 1.9 multiply_reduce_fusion
  227.9 1.0 convolution_convert_fusion.4
  229.1 21.5 %all_to_all.9 = bf16[8,5,4096]{2,1,0:T(8,128)(2,1)S(1)} all-to-all(bf16[8,5,4096]{2,1,0:T(8,128)(2,1)S(1)} %reshape.53), channel_id=1, replica_groups=mesh['branch'=8,'mp'=8,'dp'=4] {'branch'}, dimensions={0} | all-to-all | bytes 655360 | tf_op jit(solution)/shard_map/all_to_all | solution.py:99
  250.5 0.9 squeeze.27
  251.5 8.6 %fusion.9 = f32[1280,172]{0,1:T(8,128)} fusion(bf16[1280,4096]{1,0:T(8,128)(2,1)} %all-gather.8.cloned.1.call-done, bf16[1,172,4096]{2,1,0:T(8,128)(2,1)S(1)} %copy-done), kind=kOutput, calls=%fused_computation.19 | convolution fusion | flops 1803550720 | bytes 12775424 | tf_op jit(solution)/shard_map/dot_general | solution.py:25
  260.1 61.2 %all-gather.6.cloned.1.call-done = bf16[1280,4096]{1,0:T(8,128)(2,1)} async-done(((bf16[40,4096]{1,0:T(8,128)(2,1)}), bf16[1280,4096]{1,0:T(8,128)(2,1)}) %all-gather.6.cloned.1.call-update) | async-done | bytes 10485776 | tf_op jit(solution)/shard_map/all_gather | solution.py:105
  321.3 7.8 %fusion.5 = f32[1280,172]{0,1:T(8,128)S(1)} fusion(bf16[1280,4096]{1,0:T(8,128)(2,1)} %all-gather.6.cloned.1.call-done, bf16[1,4096,172]{1,2,0:T(8,128)(2,1)S(1)} %copy-done.9), kind=kOutput, calls=%fused_computation.15 | convolution fusion | flops 1803550720 | bytes 12775424 | tf_op jit(solution)/shard_map/dot_general | solution.py:20
  329.1 7.8 %fusion.7 = f32[1280,172]{0,1:T(8,128)S(1)} fusion(bf16[1280,4096]{1,0:T(8,128)(2,1)} %all-gather.6.cloned.1.call-done, bf16[1,4096,172]{1,2,0:T(8,128)(2,1)S(1)} %copy-done.10), kind=kOutput, calls=%fused_computation.17 | convolution fusion | flops 1803550720 | bytes 12775424 | tf_op jit(solution)/shard_map/dot_general | solution.py:21
  336.9 3.2 fusion.2
  340.2 3.5 fusion
  343.7 3.3 fusion.1
  (63 shorter events, 1.0 us)
Async XLA Ops:
  8.0 243.5 %copy-start = (bf16[1,172,4096]{2,1,0:T(8,128)(2,1)S(1)}, bf16[1,172,4096]{2,1,0:T(8,128)(2,1)}, u32[]{:S(2)}) copy-start(bf16[1,172,4096]{2,1,0:T(8,128)(2,1)} %param.16) | copy-start | bytes 4227076
  8.0 78.6 %all-reduce.3.cloned.1.call-start = ((), (), s32[]{:S(2)}) async-start(), calls=%async_computation.2 | async-start | bytes 2097152 | tf_op jit(solution)/shard_map/psum | solution.py:52
  8.1 81.0 %copy-start.7 = (s32[128,2]{0,1:T(2,128)S(1)}, s32[128,2]{0,1:T(2,128)}, u32[]{:S(2)}) copy-start(s32[128,2]{0,1:T(2,128)} %param.18) | copy-start | bytes 3076
  8.1 82.0 %copy-start.8 = (s32[128,2]{0,1:T(2,128)S(1)}, s32[128,2]{0,1:T(2,128)}, u32[]{:S(2)}) copy-start(s32[128,2]{0,1:T(2,128)} %param.19) | copy-start | bytes 3076
  8.1 125.4 %copy-start.4 = (bf16[128,512]{1,0:T(8,128)(2,1)S(1)}, bf16[128,512]{1,0:T(8,128)(2,1)}, u32[]{:S(2)}) copy-start(bf16[128,512]{1,0:T(8,128)(2,1)} %param.10) | copy-start | bytes 393220
  8.7 124.7 %all-gather.4.cloned.1.call-start = ((), (), s32[]{:S(2)}) async-start(), calls=%async_computation.3 | async-start | bytes 5242880 | tf_op jit(solution)/shard_map/all_gather | solution.py:58
  89.0 137.0 %all-reduce.5.cloned.1.call-start = ((), (), s32[]{:S(2)}) async-start(), calls=%async_computation.4 | async-start | bytes 2097152 | tf_op jit(solution)/shard_map/psum | solution.py:61
  90.1 48.0 %copy-start.2 = (bf16[128,4096]{1,0:T(8,128)(2,1)S(1)}, bf16[128,4096]{1,0:T(8,128)(2,1)}, u32[]{:S(2)}) copy-start(bf16[128,4096]{1,0:T(8,128)(2,1)} %param.17) | copy-start | bytes 3145732
  138.0 113.5 %all-gather.8.cloned.1.call-start = ((), (), s32[]{:S(2)}) async-start(), calls=%async_computation.6 | async-start | bytes 10813440 | tf_op jit(solution)/shard_map/all_gather | solution.py:106
  138.2 25.4 %copy-start.6 = (bf16[4096]{0:T(1024)(128)(2,1)S(1)}, bf16[4096]{0:T(1024)(128)(2,1)}, u32[]{:S(2)}) copy-start(bf16[4096]{0:T(1024)(128)(2,1)} %param.13) | copy-start | bytes 24580
  138.5 25.7 %copy-start.3 = (bf16[128,4096]{1,0:T(8,128)(2,1)S(1)}, bf16[128,4096]{1,0:T(8,128)(2,1)}, u32[]{:S(2)}) copy-start(bf16[128,4096]{1,0:T(8,128)(2,1)} %param.11) | copy-start | bytes 3145732
  163.5 157.8 %all-gather.6.cloned.1.call-start = ((), (), s32[]{:S(2)}) async-start(), calls=%async_computation.5 | async-start | bytes 10813440 | tf_op jit(solution)/shard_map/all_gather | solution.py:105
  164.9 63.0 %copy-start.5 = (f32[4096]{0:T(1024)S(1)}, f32[4096]{0:T(1024)}, u32[]{:S(2)}) copy-start(f32[4096]{0:T(1024)} %convert_element_type.69) | copy-start | bytes 49156
  226.0 1.9 copy-start.1
  251.4 69.9 %copy-start.9 = (bf16[1,4096,172]{1,2,0:T(8,128)(2,1)S(1)}, bf16[1,4096,172]{1,2,0:T(8,128)(2,1)}, u32[]{:S(2)}) copy-start(bf16[1,4096,172]{1,2,0:T(8,128)(2,1)} %param.14) | copy-start | bytes 4227076
  321.3 7.8 %copy-start.10 = (bf16[1,4096,172]{1,2,0:T(8,128)(2,1)S(1)}, bf16[1,4096,172]{1,2,0:T(8,128)(2,1)}, u32[]{:S(2)}) copy-start(bf16[1,4096,172]{1,2,0:T(8,128)(2,1)} %param.15) | copy-start | bytes 4227076
  321.3 15.6 %slice-start = ((s8[10485760]{0:T(1024)(128)(4,1)}), s8[4194304]{0:T(1024)(128)(4,1)S(1)}, s32[]{:S(2)}) async-start(s8[10485760]{0:T(1024)(128)(4,1)} %bitcast.46), calls=%async_computation.7 | async-start | bytes 8388608
  321.3 15.6 %slice-start.1 = ((s8[10485760]{0:T(1024)(128)(4,1)}), s8[4194304]{0:T(1024)(128)(4,1)S(1)}, s32[]{:S(2)}) async-start(s8[10485760]{0:T(1024)(128)(4,1)} %bitcast.46), calls=%async_computation.8 | async-start | bytes 8388608
  329.1 7.8 %slice-start.2 = ((s8[10485760]{0:T(1024)(128)(4,1)}), s8[2097152]{0:T(1024)(128)(4,1)S(1)}, s32[]{:S(2)}) async-start(s8[10485760]{0:T(1024)(128)(4,1)} %bitcast.46), calls=%async_computation.9 | async-start | bytes 4194304
  329.1 11.1 %slice-start.3 = ((s8[10485760]{0:T(1024)(128)(4,1)}), s8[4194304]{0:T(1024)(128)(4,1)S(1)}, s32[]{:S(2)}) async-start(s8[10485760]{0:T(1024)(128)(4,1)} %bitcast.48), calls=%async_computation.10 | async-start | bytes 8388608
  329.1 11.1 %slice-start.4 = ((s8[10485760]{0:T(1024)(128)(4,1)}), s8[4194304]{0:T(1024)(128)(4,1)S(1)}, s32[]{:S(2)}) async-start(s8[10485760]{0:T(1024)(128)(4,1)} %bitcast.48), calls=%async_computation.11 | async-start | bytes 8388608
  336.9 3.3 slice-start.5
  336.9 3.3 copy-start.11
Sparse Core Ops, SparseCore 0:
  11.2 75.3 all-reduce.2
  89.1 44.2 all-gather.3
  138.1 87.8 all-reduce.4
Sparse Core Ops, SparseCore 1:
  163.6 76.4 all-gather.7
  251.5 69.8 all-gather.5
where the time goes:
time: 354 us
  waiting for transfers between devices  244 us (69%)
  blocking collectives  45.5 us (13%)
  matrix products  40 us (11%)
  between operations  15.5 us (4%)
  other arithmetic  5.78 us (2%)
    psum x1, waiting for transfers between devices, per_device(): lax.psum(attn_weight[0].astype(jnp.float32).astype(jnp.bfloat16), 'branch')  77.8 us
    all_gather x1, waiting for transfers between devices, per_device(): lax.all_gather(routed_in[0], ('mp', 'dp'), axis=0, tiled=True)  61.2 us
    psum x1, waiting for transfers between devices, per_device(): lax.psum(partial_out.astype(jnp.float32).astype(jnp.bfloat16), 'mp')  61.1 us
    all_gather x1, waiting for transfers between devices, per_device(): lax.all_gather(merged, 'dp', axis=1, tiled=True)  43.3 us
    all_to_all x1, blocking collectives, per_device(): lax.all_to_all(send_cot, 'branch', split_axis=0, concat_axis=1, tiled=True)  24 us
    all_to_all x1, blocking collectives, per_device(): lax.all_to_all(send_in, 'branch', split_axis=0, concat_axis=1, tiled=True)  21.5 us
    dot_general x1, matrix products, expert_pass(): lax.dot_general(cotan_rows, w_down, (((1,), (1,)), ((), ())), preferred_e...  8.63 us
    dot_general x1, matrix products, expert_pass(): pre_gate = jnp.dot(tokens_in, w_gate, preferred_element_type=jnp.float32)  7.76 us
  transfers between devices with their start and end apart: 5, of which 4 were waited for; matrix products, arithmetic and copies ran while one was open for 5% of the time, Pallas kernels for 0%

commit v1 on v0

--- a/solution.py
+++ b/solution.py
@@ -3,6 +3,13 @@
 import jax.numpy as jnp
 from jax import lax
 from jax.sharding import PartitionSpec as P
+
+
+def swapped_in(array, name, d):
+    size = lax.axis_size(name)
+    shards = jnp.stack([array for _ in range(size)])
+    shards = lax.all_to_all(shards, name, split_axis=0, concat_axis=0)
+    return jnp.concatenate(shards, axis=d)
 
 
 def slot_positions(id_block, capacity, experts):
@@ -102,7 +109,7 @@
     totals = accumulate(
         start_totals,
         (
-            lax.all_gather(routed_in[0], ("mp", "dp"), axis=0, tiled=True),
+            swapped_in(routed_in[0], ("mp", "dp"), 0),
             lax.all_gather(routed_cot[0], ("mp", "dp"), axis=0, tiled=True),
         ),
         jnp.int32(0),

time: 354 us -> 413 us (1.17)
  blocking collectives: 45.5 us -> 173 us
  waiting for transfers between devices: 244 us -> 183 us
  matrix products: 40 us -> 32.6 us
    all_to_all x0 -> x1, blocking collectives: none -> 128 us  [swapped_in(): shards = lax.all_to_all(shards, name, split_axis=0, concat_axis=0)]
    all_gather x1 -> x0, waiting for transfers between devices: 61.2 us -> none  [per_device(): lax.all_gather(routed_in[0], ('mp', 'dp'), axis=0, tiled=True)]
  transfers between devices with their start and end apart: 5 -> 4, of which waited for: 4 -> 3; matrix products, arithmetic and copies ran while one was open for 5% -> 4% of each run, Pallas kernels for 0% -> 0%
where the time goes in v1:
time: 413 us
  waiting for transfers between devices  183 us (44%)
  blocking collectives  173 us (42%)
  matrix products  32.6 us (8%)
  between operations  15.5 us (4%)
  other arithmetic  5.17 us (1%)
    all_to_all x1, blocking collectives, swapped_in(): shards = lax.all_to_all(shards, name, split_axis=0, concat_axis=0)  128 us
    psum x1, waiting for transfers between devices, per_device(): lax.psum(attn_weight[0].astype(jnp.float32).astype(jnp.bfloat16), 'branch')  77.8 us
    psum x1, waiting for transfers between devices, per_device(): lax.psum(partial_out.astype(jnp.float32).astype(jnp.bfloat16), 'mp')  60.9 us
    all_gather x1, waiting for transfers between devices, per_device(): lax.all_gather(merged, 'dp', axis=1, tiled=True)  43.3 us
    all_to_all x1, blocking collectives, per_device(): lax.all_to_all(send_cot, 'branch', split_axis=0, concat_axis=1, tiled=True)  24 us
    all_to_all x1, blocking collectives, per_device(): lax.all_to_all(send_in, 'branch', split_axis=0, concat_axis=1, tiled=True)  21 us
  transfers between devices with their start and end apart: 4, of which 3 were waited for; matrix products, arithmetic and copies ran while one was open for 4% of the time, Pallas kernels for 0%

profile of v1, /device:TPU:1, one launch (start us, length us, event | category | flops | bytes accessed | tf_op | source)
XLA Modules:
  0.0 412.9 jit_solution(11387495929308807610)
XLA Ops:
  8.1 0.7 all-reduce.3.cloned.1.call-update
  8.8 77.8 %all-reduce.3.cloned.1.call-done = bf16[512,1024]{1,0:T(8,128)(2,1)} async-done(((bf16[512,1024]{1,0:T(8,128)(2,1)}), bf16[512,1024]{1,0:T(8,128)(2,1)}) %all-reduce.3.cloned.1.call-update) | async-done | bytes 1048592 | tf_op jit(solution)/shard_map/psum | solution.py:59
  86.6 2.4 multiply_convert_fusion.1
  89.1 0.6 reduce-window.6
  89.7 0.2 slice_reduce_fusion
  90.1 43.3 %all-gather.3.cloned.1.call-done = bf16[512,4096]{1,0:T(8,128)(2,1)} async-done(((bf16[512,1024]{1,0:T(8,128)(2,1)}), bf16[512,4096]{1,0:T(8,128)(2,1)}) %all-gather.3.cloned.1.call-update) | async-done | bytes 4194320 | tf_op jit(solution)/shard_map/all_gather | solution.py:65
  133.5 4.5 %fusion.3 = bf16[128,4096]{0,1:T(8,128)(2,1)} fusion(bf16[512,4096]{1,0:T(8,128)(2,1)} %all-gather.3.cloned.1.call-done, bf16[128,512]{1,0:T(8,128)(2,1)S(1)} %copy-done.6), kind=kOutput, calls=%fused_computation.7 | convolution fusion | flops 537395200 | bytes 5373952 | tf_op jit(solution)/shard_map/dot_general | solution.py:63
  138.2 0.3 fusion.4
  138.6 24.0 %all_to_all.26 = bf16[8,5,4096]{2,1,0:T(8,128)(2,1)S(1)} all-to-all(bf16[8,5,4096]{2,1,0:T(8,128)(2,1)S(1)} %reshape.59), channel_id=1, replica_groups=mesh['branch'=8,'mp'=8,'dp'=4] {'branch'}, dimensions={0} | all-to-all | bytes 655360 | tf_op jit(solution)/shard_map/all_to_all | solution.py:107
  162.6 0.9 squeeze.24
  163.5 0.7 copy.19
  164.2 60.9 %all-reduce.5.cloned.1.call-done = bf16[128,4096]{0,1:T(8,128)(2,1)} async-done(((bf16[128,4096]{0,1:T(8,128)(2,1)}), bf16[128,4096]{0,1:T(8,128)(2,1)}) %all-reduce.5.cloned.1.call-update) | async-done | bytes 1048592 | tf_op jit(solution)/shard_map/psum | solution.py:68
  225.1 1.9 multiply_reduce_fusion
  227.0 1.0 convolution_convert_fusion.4
  228.2 21.0 %all_to_all.27 = bf16[8,5,4096]{2,1,0:T(8,128)(2,1)S(1)} all-to-all(bf16[8,5,4096]{2,1,0:T(8,128)(2,1)S(1)} %reshape.57), channel_id=1, replica_groups=mesh['branch'=8,'mp'=8,'dp'=4] {'branch'}, dimensions={0} | all-to-all | bytes 655360 | tf_op jit(solution)/shard_map/all_to_all | solution.py:106
  249.1 0.1 all_to_all.9
  249.3 1.3 stack.15
  250.6 128.2 %all_to_all.28 = bf16[32,40,4096]{2,1,0:T(8,128)(2,1)S(1)} all-to-all(bf16[32,40,4096]{2,1,0:T(8,128)(2,1)S(1)} %stack.15), channel_id=1, replica_groups=mesh['branch'=8,'mp'=8,'dp'=4] {'mp','dp'}, dimensions={0} | all-to-all | bytes 20971520 | tf_op jit(solution)/shard_map/all_to_all | solution.py:11
  378.8 4.5 %fusion.5 = f32[1280,172]{0,1:T(8,128)} fusion(bf16[1280,4096]{1,0:T(8,128)(2,1)S(1)} %bitcast.46, bf16[1,4096,172]{1,2,0:T(8,128)(2,1)S(1)} %copy-done), kind=kOutput, calls=%fused_computation.15 | convolution fusion | flops 1803550720 | bytes 12775424 | tf_op jit(solution)/shard_map/dot_general | solution.py:27
  383.3 4.5 %fusion.7 = f32[1280,172]{0,1:T(8,128)} fusion(bf16[1280,4096]{1,0:T(8,128)(2,1)S(1)} %bitcast.47, bf16[1,4096,172]{1,2,0:T(8,128)(2,1)S(1)} %copy-done.10), kind=kOutput, calls=%fused_computation.17 | convolution fusion | flops 1803550720 | bytes 12775424 | tf_op jit(solution)/shard_map/dot_general | solution.py:28
  387.9 7.8 %fusion.9 = f32[1280,172]{0,1:T(8,128)S(1)} fusion(bf16[1280,4096]{1,0:T(8,128)(2,1)} %all-gather.5.cloned.1.call-done, bf16[1,172,4096]{2,1,0:T(8,128)(2,1)S(1)} %copy-done.11), kind=kOutput, calls=%fused_computation.19 | convolution fusion | flops 1803550720 | bytes 12775424 | tf_op jit(solution)/shard_map/dot_general | solution.py:32
  395.7 3.3 fusion.1
  399.0 3.5 fusion
  402.5 3.2 fusion.2
  (59 shorter events, 0.9 us)
Async XLA Ops:
  8.0 370.8 %copy-start = (bf16[1,4096,172]{1,2,0:T(8,128)(2,1)S(1)}, bf16[1,4096,172]{1,2,0:T(8,128)(2,1)}, u32[]{:S(2)}) copy-start(bf16[1,4096,172]{1,2,0:T(8,128)(2,1)} %param.14) | copy-start | bytes 4227076
  8.0 78.6 %all-reduce.3.cloned.1.call-start = ((), (), s32[]{:S(2)}) async-start(), calls=%async_computation.3 | async-start | bytes 2097152 | tf_op jit(solution)/shard_map/psum | solution.py:59
  8.1 81.0 %copy-start.8 = (s32[128,2]{0,1:T(2,128)S(1)}, s32[128,2]{0,1:T(2,128)}, u32[]{:S(2)}) copy-start(s32[128,2]{0,1:T(2,128)} %param.18) | copy-start | bytes 3076
  8.1 82.0 %copy-start.9 = (s32[128,2]{0,1:T(2,128)S(1)}, s32[128,2]{0,1:T(2,128)}, u32[]{:S(2)}) copy-start(s32[128,2]{0,1:T(2,128)} %param.19) | copy-start | bytes 3076
  8.1 125.4 %copy-start.6 = (bf16[128,512]{1,0:T(8,128)(2,1)S(1)}, bf16[128,512]{1,0:T(8,128)(2,1)}, u32[]{:S(2)}) copy-start(bf16[128,512]{1,0:T(8,128)(2,1)} %param.10) | copy-start | bytes 393220
  8.7 124.7 %all-gather.3.cloned.1.call-start = ((), (), s32[]{:S(2)}) async-start(), calls=%async_computation.4 | async-start | bytes 5242880 | tf_op jit(solution)/shard_map/all_gather | solution.py:65
  89.0 136.1 %all-reduce.5.cloned.1.call-start = ((), (), s32[]{:S(2)}) async-start(), calls=%async_computation.5 | async-start | bytes 2097152 | tf_op jit(solution)/shard_map/psum | solution.py:68
  90.1 48.0 %copy-start.4 = (bf16[128,4096]{1,0:T(8,128)(2,1)S(1)}, bf16[128,4096]{1,0:T(8,128)(2,1)}, u32[]{:S(2)}) copy-start(bf16[128,4096]{1,0:T(8,128)(2,1)} %param.17) | copy-start | bytes 3145732
  138.0 249.9 %all-gather.5.cloned.1.call-start = ((), (), s32[]{:S(2)}) async-start(), calls=%async_computation.6 | async-start | bytes 10813440 | tf_op jit(solution)/shard_map/all_gather | solution.py:113
  138.4 25.1 %copy-start.5 = (bf16[128,4096]{1,0:T(8,128)(2,1)S(1)}, bf16[128,4096]{1,0:T(8,128)(2,1)}, u32[]{:S(2)}) copy-start(bf16[128,4096]{1,0:T(8,128)(2,1)} %param.11) | copy-start | bytes 3145732
  138.6 25.6 %copy-start.7 = (bf16[4096]{0:T(1024)(128)(2,1)S(1)}, bf16[4096]{0:T(1024)(128)(2,1)}, u32[]{:S(2)}) copy-start(bf16[4096]{0:T(1024)(128)(2,1)} %param.13) | copy-start | bytes 24580
  225.1 1.9 copy-start.3
  378.8 4.5 %copy-start.1 = (bf16[32,40,4096]{2,1,0:T(8,128)(2,1)}, bf16[32,40,4096]{2,1,0:T(8,128)(2,1)S(1)}, u32[]{:S(2)}) copy-start(bf16[32,40,4096]{2,1,0:T(8,128)(2,1)S(1)} %all_to_all.28) | copy-start | bytes 31457284
  378.8 4.5 %copy-start.10 = (bf16[1,4096,172]{1,2,0:T(8,128)(2,1)S(1)}, bf16[1,4096,172]{1,2,0:T(8,128)(2,1)}, u32[]{:S(2)}) copy-start(bf16[1,4096,172]{1,2,0:T(8,128)(2,1)} %param.15) | copy-start | bytes 4227076
  383.3 4.5 %copy-start.11 = (bf16[1,172,4096]{2,1,0:T(8,128)(2,1)S(1)}, bf16[1,172,4096]{2,1,0:T(8,128)(2,1)}, u32[]{:S(2)}) copy-start(bf16[1,172,4096]{2,1,0:T(8,128)(2,1)} %param.16) | copy-start | bytes 4227076
  387.8 7.8 %copy-start.2 = (bf16[32,40,4096]{2,1,0:T(8,128)(2,1)S(1)}, bf16[32,40,4096]{2,1,0:T(8,128)(2,1)}, u32[]{:S(2)}) copy-start(bf16[32,40,4096]{2,1,0:T(8,128)(2,1)} %copy-done.1) | copy-start | bytes 31457284
  387.9 7.8 %copy-start.12 = (f32[1280,172]{0,1:T(8,128)S(1)}, f32[1280,172]{0,1:T(8,128)}, u32[]{:S(2)}) copy-start(f32[1280,172]{0,1:T(8,128)} %fusion.5) | copy-start | bytes 2641924
  395.6 3.3 copy-start.13
  395.6 6.9 %slice-start = ((s8[10485760]{0:T(1024)(128)(4,1)}), s8[4194304]{0:T(1024)(128)(4,1)S(1)}, s32[]{:S(2)}) async-start(s8[10485760]{0:T(1024)(128)(4,1)} %bitcast.51), calls=%async_computation.7 | async-start | bytes 8388608
  395.7 6.8 %slice-start.1 = ((s8[10485760]{0:T(1024)(128)(4,1)}), s8[4194304]{0:T(1024)(128)(4,1)S(1)}, s32[]{:S(2)}) async-start(s8[10485760]{0:T(1024)(128)(4,1)} %bitcast.51), calls=%async_computation.8 | async-start | bytes 8388608
  399.0 3.5 slice-start.2
Sparse Core Ops, SparseCore 0:
  11.2 75.3 all-reduce.2
  89.1 44.2 all-gather.2
  138.1 86.9 all-reduce.4
Sparse Core Ops, SparseCore 1:
  163.6 76.5 all-gather.4
